TPU v7x, 32 devices: a whole 2x2x4 slice. The times are simulated.
32 devices in a mesh: dp: 8 (over z, y), chan: 4 (over x, core).
Axes of the slice: x: 2, y: 2, z: 4, core: 2. Of those that a mesh axis runs over, the one named last changes fastest.
Arguments:
- activations: bfloat16 [8, 16, 64, 1024], P('dp', None, None, 'chan'), may hold values from -60 to 60
- cotangent: bfloat16 [8, 16, 64, 1024], P('dp', None, None, 'chan'), may hold values from -6 to 6
- dw_kernel: float32 [49, 1024], P(None, 'chan'), may hold values from -0.875 to 0.875
- norm_gain: float32 [4, 1024], P(None, 'chan'), may hold values from 0.1 to 1.9
- norm_bias: float32 [4, 1024], P(None, 'chan'), may hold values from -3 to 3
- w_in: bfloat16 [1024, 4096], P(None, 'chan'), may hold values from -0.1875 to 0.1875
- b_in: float32 [4096], P('chan'), may hold values from -3 to 3
- w_out: bfloat16 [4096, 1024], P('chan'), may hold values from -0.09375 to 0.09375
- layer_scale: float32 [1024], P('chan'), may hold values from 0.3 to 1.5
- group_sizes: int32 [4], replicated, may hold values from 1 to 4, 8 in all
Outputs:
- result: bfloat16 [8, 16, 64, 1024], P('dp', None, None, 'chan')
- d_input: bfloat16 [8, 16, 64, 1024], P('dp', None, None, 'chan')
- d_kernel: float32 [49, 1024], P(None, 'chan')
- d_gain: float32 [4, 1024], P(None, 'chan')
- d_bias: float32 [4, 1024], P(None, 'chan')
- d_w_in: float32 [1024, 4096], P('dp', 'chan')
- d_b_in: float32 [4096], P('chan')
- d_w_out: float32 [4096, 1024], P('chan', 'dp')
- d_scale: float32 [1024], P('chan')
Inputs may be any that keep to these rules, and one draw needn't show every extreme that they name: `group_sizes`: the sizes sum to 8, each is at least one, and the largest is exactly 4.
All inputs are finite; a program needn't handle non-finite values.
Results may differ from a plain program's by a relative error of at most 0.015.
Values may be sent and summed in bfloat16 or wider, within the bound.
A program may use at most 128 MiB of HBM per device.

v0:
```python
import jax
import jax.numpy as jnp
from jax import lax
from jax.sharding import PartitionSpec as P

KS = 7
EPS = 1e-05


def depthwise(field, kernel):
    reach = KS // 2
    height, width = (field.shape[1], field.shape[2])
    padded = jnp.pad(field, ((0, 0), (reach, reach), (reach, reach), (0, 0)))
    running = jnp.zeros(field.shape, jnp.float32)
    for shift_row in range(KS):
        for shift_col in range(KS):
            window = padded[:, shift_row : shift_row + height, shift_col : shift_col + width, :]
            running = running + window * kernel[shift_row * KS + shift_col]
    return running


def kernel_grad(field, upstream):
    reach = KS // 2
    height, width = (field.shape[1], field.shape[2])
    padded = jnp.pad(field, ((0, 0), (reach, reach), (reach, reach), (0, 0)))
    collected = []
    for shift_row in range(KS):
        for shift_col in range(KS):
            window = padded[:, shift_row : shift_row + height, shift_col : shift_col + width, :]
            collected.append(jnp.sum(window * upstream, axis=(0, 1, 2)))
    return jnp.stack(collected)


def group_owners(group_sizes, number):
    group_ends = jnp.cumsum(group_sizes)
    positions = jnp.arange(number, dtype=jnp.int32)
    labels = jnp.sum((group_ends[None, :] <= positions[:, None]).astype(jnp.int32), axis=1)
    return (jnp.arange(group_sizes.shape[0], dtype=jnp.int32)[:, None] == labels[None, :]).astype(
        jnp.float32
    )


def body(
    activations,
    cotangent,
    dw_kernel,
    norm_gain,
    norm_bias,
    w_in,
    b_in,
    w_out,
    layer_scale,
    group_sizes,
):
    height, width, channels = (activations.shape[1], activations.shape[2], activations.shape[3])
    row_count = height * width
    devices = lax.axis_size("dp")
    position = lax.axis_index("dp")
    group_ends = jnp.cumsum(group_sizes)
    own_group = jnp.sum((group_ends <= position).astype(jnp.int32))
    member = (jnp.arange(group_sizes.shape[0], dtype=jnp.int32) == own_group).astype(jnp.float32)
    counts = group_sizes.astype(jnp.float32) * row_count
    own_count = jnp.sum(member * counts)
    source = activations.astype(jnp.float32)
    filtered = depthwise(source, dw_kernel).reshape(row_count, channels)
    moments = jnp.stack([jnp.sum(filtered, axis=0), jnp.sum(filtered * filtered, axis=0)])
    per_device = lax.all_gather(moments[None], "dp", axis=0, tiled=True)
    owners = group_owners(group_sizes, devices)
    totals = jnp.sum(owners[:, :, None, None] * per_device[None], axis=1)
    group_mean = totals[:, 0] / counts[:, None]
    group_var = totals[:, 1] / counts[:, None] - group_mean * group_mean
    group_rstd = lax.rsqrt(group_var + EPS)
    own_mean = jnp.sum(member[:, None] * group_mean, axis=0)
    own_rstd = jnp.sum(member[:, None] * group_rstd, axis=0)
    own_gain = jnp.sum(member[:, None] * norm_gain, axis=0)
    own_bias = jnp.sum(member[:, None] * norm_bias, axis=0)
    centered = (filtered - own_mean) * own_rstd
    normed = (centered * own_gain + own_bias).astype(jnp.bfloat16)
    gathered = lax.all_gather(normed, "chan", axis=1, tiled=True)
    hidden = jnp.dot(gathered, w_in, preferred_element_type=jnp.float32) + b_in
    activated = jax.nn.gelu(hidden).astype(jnp.bfloat16)
    partial_branch = jnp.dot(activated, w_out, preferred_element_type=jnp.float32)
    branch = lax.psum_scatter(
        partial_branch.astype(jnp.bfloat16), "chan", scatter_dimension=1, tiled=True
    ).astype(jnp.float32)
    initial = source.reshape(row_count, channels)
    result = (initial + layer_scale * branch).astype(jnp.bfloat16).reshape(activations.shape)
    incoming = cotangent.reshape(row_count, channels).astype(jnp.float32)
    scale_local = jnp.sum(incoming * branch, axis=0)
    d_branch = (incoming * layer_scale).astype(jnp.bfloat16)
    branch_full = lax.all_gather(d_branch, "chan", axis=1, tiled=True)
    contract_rows = (((0,), (0,)), ((), ()))
    contract_cols = (((1,), (1,)), ((), ()))
    out_local_t = lax.dot_general(
        branch_full, activated, contract_rows, preferred_element_type=jnp.float32
    )
    d_activated = lax.dot_general(
        branch_full, w_out, contract_cols, preferred_element_type=jnp.float32
    )
    _, pullback = jax.vjp(jax.nn.gelu, hidden)
    d_hidden = pullback(d_activated)[0]
    bias_local = jnp.sum(d_hidden, axis=0)
    hidden_b = d_hidden.astype(jnp.bfloat16)
    in_local = lax.dot_general(
        gathered, hidden_b, contract_rows, preferred_element_type=jnp.float32
    )
    hidden_cols = in_local.shape[1]
    both_local = jnp.concatenate([in_local, out_local_t], axis=1)
    both_sums = lax.psum_scatter(
        both_local.astype(jnp.bfloat16), "dp", scatter_dimension=0, tiled=True
    ).astype(jnp.float32)
    d_w_in = both_sums[:, :hidden_cols]
    d_w_out = both_sums[:, hidden_cols:].T
    partial_normed = lax.dot_general(
        hidden_b, w_in, contract_cols, preferred_element_type=jnp.float32
    )
    d_normed = lax.psum_scatter(
        partial_normed.astype(jnp.bfloat16), "chan", scatter_dimension=1, tiled=True
    ).astype(jnp.float32)
    grad_moments = jnp.stack([jnp.sum(d_normed * centered, axis=0), jnp.sum(d_normed, axis=0)])
    grad_rows = lax.all_gather(grad_moments[None], "dp", axis=0, tiled=True)
    grad_owners = group_owners(group_sizes, devices)
    grad_totals = jnp.sum(grad_owners[:, :, None, None] * grad_rows[None], axis=1)
    d_gain = grad_totals[:, 0]
    d_bias = grad_totals[:, 1]
    own_dgain = jnp.sum(member[:, None] * d_gain, axis=0)
    own_dbias = jnp.sum(member[:, None] * d_bias, axis=0)
    d_filtered = (
        own_gain * own_rstd * (d_normed - own_dbias / own_count - centered * own_dgain / own_count)
    )
    d_filtered = d_filtered.reshape(activations.shape)
    kernel_local = kernel_grad(source, d_filtered)
    d_kernel, d_b_in, d_scale = lax.psum((kernel_local, bias_local, scale_local), "dp")
    d_input = (cotangent.astype(jnp.float32) + depthwise(d_filtered, dw_kernel[::-1])).astype(
        jnp.bfloat16
    )
    return (result, d_input, d_kernel, d_gain, d_bias, d_w_in, d_b_in, d_w_out, d_scale)


def solution(mesh):
    in_specs = (
        P("dp", None, None, "chan"),
        P("dp", None, None, "chan"),
        P(None, "chan"),
        P(None, "chan"),
        P(None, "chan"),
        P(None, "chan"),
        P("chan"),
        P("chan", None),
        P("chan"),
        P(),
    )
    out_specs = (
        P("dp", None, None, "chan"),
        P("dp", None, None, "chan"),
        P(None, "chan"),
        P(None, "chan"),
        P(None, "chan"),
        P("dp", "chan"),
        P("chan"),
        P("chan", "dp"),
        P("chan"),
    )
    return jax.shard_map(body, mesh=mesh, in_specs=in_specs, out_specs=out_specs, check_vma=False)
```

profile of v0, /device:TPU:0, one launch (start us, length us, event | category | flops | bytes accessed | tf_op | source)
XLA Modules:
  0.0 303.6 jit_solution(11111486553160216814)
XLA Ops:
  7.2 0.0 copy-start
  7.2 0.0 copy-start.5
  7.2 0.0 copy-start.4
  7.2 0.0 all-gather.7.cloned.1.call-start
  7.3 1.0 reduce-window.8
  8.2 0.6 fusion.117
  8.9 0.6 compare_convert_fusion.1
  9.5 1.9 fusion.116
  11.4 0.9 fusion.124
  12.4 1.1 fusion.122
  13.4 1.1 fusion.123
  14.6 0.1 convert_reduce_fusion.1
  14.7 1.1 convert_element_type.75
  15.8 9.7 %fusion.118 = (f32[256]{0:T(256)S(1)}, f32[256]{0:T(256)S(1)}, f32[1,16,64,256]{3,2,1,0:T(8,128)}) fusion(f32[256]{0:T(256)S(1)} %bitcast.229, f32[256]{0:T(256)S(1)} %bitcast.231, f32[256]{0:T(256)S(1)} %bitcast.235, f32[256]{0:T(256)S(1)} %bitcast.237, f32[256]{0:T(256)S(1)} %bitcast.239, f32[256]{0:T(256)S(1)} %bitcast.241, f32[256]{0:T(256)S(1)} %bitcast.243, ...), kind=kLoop, calls=%fused_computation.304 | loop fusion | flops 26213888 | bytes 2149376 | tf_op jit(solution)/shard_map/reduce_sum | solution.py:66
  25.5 27.9 %all-gather.2 = f32[8,2,256]{2,1,0:T(2,128)S(1)} all-gather(f32[1,2,256]{2,1,0:T(2,128)S(1)} %maximum_bitcast_fusion), channel_id=2, replica_groups=mesh['dp'=8,'chan'=4] {'dp'}, dimensions={0}, use_global_device_ids=true | all-gather | bytes 18432 | tf_op jit(solution)/shard_map/all_gather | solution.py:67
  53.5 0.1 multiply_reduce_fusion.51
  53.6 0.0 copy-done.5
  53.6 0.0 copy-done.4
  53.6 0.1 multiply_reduce_fusion.57
  53.7 2.2 add_convert_fusion
  55.9 0.0 all-gather.7.cloned.1.call-update
  55.9 0.0 copy-start.9
  55.9 0.0 reduce-scatter.6.cloned.1.call-start
  56.0 22.3 %all-gather.7.cloned.1.call-done = bf16[1024,1024]{1,0:T(8,128)(2,1)} async-done(((bf16[1024,256]{1,0:T(8,128)(2,1)}), bf16[1024,1024]{1,0:T(8,128)(2,1)}) %all-gather.7.cloned.1.call-update) | async-done | bytes 2097168 | tf_op jit(solution)/shard_map/all_gather | solution.py:79
  78.3 4.6 %fusion.127 = f32[1024,1024]{1,0:T(8,128)S(1)} fusion(bf16[1024,1024]{1,0:T(8,128)(2,1)} %all-gather.7.cloned.1.call-done, bf16[1024,1024]{1,0:T(8,128)(2,1)} %param.15), kind=kOutput, calls=%fused_computation.311 | convolution fusion | flops 2147483648 | bytes 8388608 | tf_op jit(solution)/shard_map/dot_general | solution.py:80
  82.8 0.0 copy-start.10
  82.8 1.9 copy-done.10
  84.8 0.0 copy-done.9
  84.8 4.2 %convolution_convert_fusion.3 = bf16[1024,1024]{1,0:T(8,128)(2,1)} fusion(bf16[1024,1024]{1,0:T(8,128)(2,1)S(1)} %copy-done, f32[1024,1024]{1,0:T(8,128)S(1)} %fusion.127, f32[1024]{0:T(1024)S(1)} %copy-done.9), kind=kOutput, calls=%fused_computation.109 | convolution fusion | flops 2159017984 | bytes 8392704 | tf_op jit(solution)/shard_map/dot_general | solution.py:82
  88.9 0.0 reduce-scatter.6.cloned.1.call-update
  89.0 0.0 all-gather.9.cloned.1.call-start
  89.0 31.3 %reduce-scatter.6.cloned.1.call-done = bf16[1024,256]{1,0:T(8,128)(2,1)} async-done(((bf16[1024,1024]{1,0:T(8,128)(2,1)}), bf16[1024,256]{1,0:T(8,128)(2,1)}) %reduce-scatter.6.cloned.1.call-update) | async-done | bytes 524304 | tf_op jit(solution)/shard_map/reduce_scatter | solution.py:83
  120.3 2.7 fusion.8
  122.9 0.0 all-gather.9.cloned.1.call-update
  123.0 0.2 reduce-scatter.8.cloned.1.call-start
  123.2 22.7 %all-gather.9.cloned.1.call-done = bf16[1024,1024]{1,0:T(8,128)(2,1)} async-done(((bf16[1024,256]{1,0:T(8,128)(2,1)}), bf16[1024,1024]{1,0:T(8,128)(2,1)}) %all-gather.9.cloned.1.call-update) | async-done | bytes 2097168 | tf_op jit(solution)/shard_map/all_gather | solution.py:91
  145.9 7.5 %fusion.119 = (f32[1024]{0:T(1024)S(1)}, bf16[1024,1024]{1,0:T(8,128)(2,1)S(1)}) fusion(f32[1024,1024]{1,0:T(8,128)} %copy-done.10, f32[1024]{0:T(1024)S(1)} %copy-done.9, bf16[1024,1024]{1,0:T(8,128)(2,1)} %all-gather.9.cloned.1.call-done, bf16[1024,1024]{1,0:T(8,128)(2,1)S(1)} %copy-done), kind=kOutput, calls=%fused_computation.305 | convolution fusion | flops 2170551296 | bytes 10493952 | tf_op jit(solution)/shard_map/dot_general | solution.py:97
  153.4 1.3 copy-done.12
  154.7 3.8 %convolution_convert_fusion.2 = bf16[1024,1024]{1,0:T(8,128)(2,1)} fusion(bf16[1024,1024]{1,0:T(8,128)(2,1)S(1)} %copy-done.7, bf16[1024,1024]{1,0:T(8,128)(2,1)S(1)} %get-tuple-element.99), kind=kOutput, calls=%fused_computation.108 | convolution fusion | flops 2148532224 | bytes 6291456 | tf_op jit(solution)/shard_map/dot_general | solution.py:114
  158.5 0.0 reduce-scatter.8.cloned.1.call-update
  158.5 0.0 reduce-scatter.10.cloned.1.call-start
  158.6 4.8 %convolution_convert_fusion.1 = bf16[1024,1024]{0,1:T(8,128)(2,1)S(1)} fusion(bf16[1024,1024]{1,0:T(8,128)(2,1)} %all-gather.7.cloned.1.call-done, bf16[1024,1024]{1,0:T(8,128)(2,1)} %copy-done.12), kind=kOutput, calls=%fused_computation.107 | convolution fusion | flops 2148532224 | bytes 6291456 | tf_op jit(solution)/shard_map/dot_general | solution.py:104
  163.4 3.0 convolution_convert_fusion
  166.4 2.4 pad_maximum_fusion
  168.8 6.5 %copy.27 = bf16[1024,2048]{1,0:T(8,128)(2,1)} copy(bf16[1024,2048]{0,1:T(8,128)(2,1)} %pad_maximum_fusion) | data formatting | bytes 8388608
  175.3 0.0 reduce-scatter.10.cloned.1.call-update
  175.3 14.5 %reduce-scatter.8.cloned.1.call-done = bf16[1024,256]{1,0:T(8,128)(2,1)} async-done(((bf16[1024,1024]{1,0:T(8,128)(2,1)}), bf16[1024,256]{1,0:T(8,128)(2,1)}) %reduce-scatter.8.cloned.1.call-update) | async-done | bytes 524304 | tf_op jit(solution)/shard_map/reduce_scatter | solution.py:117
  189.8 1.7 fusion.9
  191.5 0.0 copy-start.3
  191.6 27.2 %all-gather.3 = f32[8,2,256]{2,1,0:T(2,128)S(1)} all-gather(f32[1,2,256]{2,1,0:T(2,128)S(1)} %maximum_bitcast_fusion.1), channel_id=3, replica_groups=mesh['dp'=8,'chan'=4] {'dp'}, dimensions={0}, use_global_device_ids=true | all-gather | bytes 18432 | tf_op jit(solution)/shard_map/all_gather | solution.py:121
  218.8 0.1 multiply_reduce_fusion.50
  218.9 0.6 multiply_reduce_fusion.53
  219.5 0.7 broadcast_divide_fusion
  220.2 4.5 %multiply_reduce_fusion.1 = (f32[256]{0:T(256)S(1)}, f32[256]{0:T(256)S(1)}, f32[256]{0:T(256)S(1)}, f32[256]{0:T(256)S(1)}, f32[256]{0:T(256)S(1)}, /*index=5*/...) fusion(f32[1,16,64,256]{3,2,1,0:T(8,128)S(1)} %convert_element_, ...), kind=kLoop, calls=%fused_computation.224 | loop fusion | flops 11529728 | bytes 3693572 | tf_op jit(solution)/shard_map/reduce_sum | solution.py:30
  224.7 1.6 multiply_reduce_fusion.2
  226.3 2.3 multiply_reduce_fusion
  228.6 0.2 stack.223
  228.8 36.8 %all-reduce.2 = (f32[49,256]{1,0:T(8,128)}, f32[1024]{0:T(1024)}, f32[256]{0:T(256)}) all-reduce(f32[49,256]{1,0:T(8,128)S(1)} %stack.223, f32[1024]{0:T(1024)S(1)} %get-tuple-element.98, f32[256]{0:T(256)S(1)} %get-tuple-element.104), channel_id=1, replica_groups=mesh['dp'=8,'chan'=4] {'dp'}, use_global_device_ids=true, to_apply=%region_67.68 | all-reduce | flops 13824 | bytes 110592 | tf_op jit(solution)/shard_map/psum | solution.py:133
  265.6 26.2 %fusion.106 = bf16[1,16,64,256]{3,2,1,0:T(8,128)(2,1)} fusion(f32[1,16,64,256]{3,2,1,0:T(8,128)} %bitcast.209, bf16[1,16,64,256]{3,2,1,0:T(8,128)(2,1)} %param.11, f32[256]{0:T(256)S(1)} %bitcast.230, f32[256]{0:T(256)S(1)} %bitcast.232, f32[256]{0:T(256)S(1)} %bitcast.236, f32[256]{0:T(256)S(1)} %bitcast.238, f32[256]{0:T(256)S(1)} %bitcast.240, ...), kind=kLoop, calls=%fused_computation.215 | loop fusion | flops 26214400 | bytes 2147328 | tf_op jit(solution)/shard_map/convert_element_type | solution.py:134
  291.8 0.0 reduce-scatter.10.cloned.1.call-done
  291.8 1.3 copy.28
  293.2 1.1 convert_element_type.94
  294.2 1.0 copy.26
  295.2 1.9 slice_bitcast_fusion
  (24 shorter events, 0.1 us)
Async XLA Ops:
  7.2 77.6 %copy-start = (bf16[1024,1024]{1,0:T(8,128)(2,1)S(1)}, bf16[1024,1024]{1,0:T(8,128)(2,1)}, u32[]{:S(2)}) copy-start(bf16[1024,1024]{1,0:T(8,128)(2,1)} %param.17) | copy-start | bytes 6291460
  7.2 46.4 %copy-start.5 = (f32[4,256]{1,0:T(4,128)S(1)}, f32[4,256]{1,0:T(4,128)}, u32[]{:S(2)}) copy-start(f32[4,256]{1,0:T(4,128)} %param.14) | copy-start | bytes 12292
  7.2 46.4 %copy-start.4 = (f32[4,256]{1,0:T(4,128)S(1)}, f32[4,256]{1,0:T(4,128)}, u32[]{:S(2)}) copy-start(f32[4,256]{1,0:T(4,128)} %param.13) | copy-start | bytes 12292
  7.2 71.1 %all-gather.7.cloned.1.call-start = ((), (), s32[]{:S(2)}) async-start(), calls=%async_computation.3 | async-start | bytes 2621440 | tf_op jit(solution)/shard_map/all_gather | solution.py:79
  55.9 28.9 %copy-start.9 = (f32[1024]{0:T(1024)S(1)}, f32[1024]{0:T(1024)}, u32[]{:S(2)}) copy-start(f32[1024]{0:T(1024)} %param.16) | copy-start | bytes 12292
  55.9 64.4 %reduce-scatter.6.cloned.1.call-start = ((), (), s32[]{:S(2)}) async-start(), calls=%async_computation.4 | async-start | bytes 2621440 | tf_op jit(solution)/shard_map/reduce_scatter | solution.py:83
  82.8 1.9 copy-start.10
  88.9 31.3 %copy-start.6 = (f32[256]{0:T(256)S(1)}, f32[256]{0:T(256)}, u32[]{:S(2)}) copy-start(f32[256]{0:T(256)} %param.18) | copy-start | bytes 3076
  89.0 57.0 %all-gather.9.cloned.1.call-start = ((), (), s32[]{:S(2)}) async-start(), calls=%async_computation.5 | async-start | bytes 2621440 | tf_op jit(solution)/shard_map/all_gather | solution.py:91
  123.0 66.9 %reduce-scatter.8.cloned.1.call-start = ((), (), s32[]{:S(2)}) async-start(), calls=%async_computation.6 | async-start | bytes 2621440 | tf_op jit(solution)/shard_map/reduce_scatter | solution.py:117
  145.9 8.8 %copy-start.7 = (bf16[1024,1024]{1,0:T(8,128)(2,1)S(1)}, bf16[1024,1024]{1,0:T(8,128)(2,1)}, u32[]{:S(2)}) copy-start(bf16[1024,1024]{1,0:T(8,128)(2,1)} %param.15) | copy-start | bytes 6291460
  153.4 1.3 copy-start.12
  158.5 133.3 %reduce-scatter.10.cloned.1.call-start = ((), (), s32[]{:S(2)}) async-start(), calls=%async_computation.7 | async-start | bytes 4718592
  158.6 4.8 %copy-start.8 = (bf16[1024,1024]{1,0:T(8,128)(2,1)S(1)}, bf16[1024,1024]{1,0:T(8,128)(2,1)}, u32[]{:S(2)}) copy-start(bf16[1024,1024]{1,0:T(8,128)(2,1)} %all-gather.9.cloned.1.call-done) | copy-start | bytes 6291460
  158.6 4.8 %copy-start.11 = (f32[1024,1024]{1,0:T(8,128)S(1)}, f32[1024,1024]{1,0:T(8,128)}, u32[]{:S(2)}) copy-start(f32[1024,1024]{1,0:T(8,128)} %copy-done.10) | copy-start | bytes 12582916
  189.8 30.3 %copy-start.1 = (f32[1,16,64,256]{3,2,1,0:T(8,128)S(1)}, f32[1,16,64,256]{3,2,1,0:T(8,128)}, u32[]{:S(2)}) copy-start(f32[1,16,64,256]{3,2,1,0:T(8,128)} %get-tuple-element.103) | copy-start | bytes 3145732
  191.5 33.1 %copy-start.3 = (bf16[1,16,64,256]{3,2,1,0:T(8,128)(2,1)S(1)}, bf16[1,16,64,256]{3,2,1,0:T(8,128)(2,1)}, u32[]{:S(2)}) copy-start(bf16[1,16,64,256]{3,2,1,0:T(8,128)(2,1)} %param.10) | copy-start | bytes 1572868
  224.6 3.9 %copy-start.2 = (f32[1024,256]{1,0:T(8,128)}, f32[1024,256]{1,0:T(8,128)S(1)}, u32[]{:S(2)}) copy-start(f32[1024,256]{1,0:T(8,128)S(1)} %get-tuple-element.100) | copy-start | bytes 3145732
Sparse Core Ops, SparseCore 0:
  56.0 22.2 all-gather.6
  89.1 31.1 reduce-scatter.5
  123.1 22.8 all-gather.8
  158.6 31.1 reduce-scatter.7
  193.3 89.9 reduce-scatter.9
where the time goes:
time: 304 us
  blocking collectives  91.9 us (30%)
  waiting for transfers between devices  90.9 us (30%)
  other arithmetic  61.3 us (20%)
  matrix products  27.7 us (9%)
  local copies, waits for them, and re-layouts  17.3 us (6%)
  between operations  14.1 us (5%)
    psum x1, blocking collectives, body(): lax.psum((kernel_local, bias_local, scale_local), 'dp')  36.8 us
    reduce_scatter x1, waiting for transfers between devices, body(): lax.psum_scatter(partial_branch.astype(jnp.bfloat16), 'chan', scatter_dim...  31.3 us
    all_gather x1, blocking collectives, body(): per_device = lax.all_gather(moments[None], 'dp', axis=0, tiled=True)  27.9 us
    all_gather x1, blocking collectives, body(): grad_rows = lax.all_gather(grad_moments[None], 'dp', axis=0, tiled=True)  27.2 us
    convert_element_type x1, other arithmetic, body(): (cotangent.astype(jnp.float32) + depthwise(d_filtered, dw_kernel[::-1]))....  26.2 us
    all_gather x1, waiting for transfers between devices, body(): branch_full = lax.all_gather(d_branch, 'chan', axis=1, tiled=True)  22.7 us
    all_gather x1, waiting for transfers between devices, body(): gathered = lax.all_gather(normed, 'chan', axis=1, tiled=True)  22.3 us
    reduce_scatter x1, waiting for transfers between devices, body(): lax.psum_scatter(partial_normed.astype(jnp.bfloat16), 'chan', scatter_dim...  14.5 us
  transfers between devices with their start and end apart: 5, of which 4 were waited for; matrix products, arithmetic and copies ran while one was open for 18% of the time, Pallas kernels for 0%

commit v1 on v0

--- a/solution.py
+++ b/solution.py
@@ -88,7 +88,8 @@
     incoming = cotangent.reshape(row_count, channels).astype(jnp.float32)
     scale_local = jnp.sum(incoming * branch, axis=0)
     d_branch = (incoming * layer_scale).astype(jnp.bfloat16)
-    branch_full = lax.all_gather(d_branch, "chan", axis=1, tiled=True)
+    parts = lax.all_gather(d_branch, "chan", axis=0, tiled=False)
+    branch_full = jnp.concatenate(parts, axis=1)
     contract_rows = (((0,), (0,)), ((), ()))
     contract_cols = (((1,), (1,)), ((), ()))
     out_local_t = lax.dot_general(

time: 304 us -> 263 us (0.87)
  waiting for transfers between devices: 90.9 us -> 58.7 us
  other arithmetic: 61.3 us -> 46.5 us
    unnamed x6, waiting for transfers between devices: 0.1 us -> 33 us
    reduce_scatter x1, waiting for transfers between devices: 31.3 us -> 0.01 us  [body(): lax.psum_scatter(partial_branch.astype(jnp.bfloat16), 'chan', scatter_dim...]
    all_gather x1, waiting for transfers between devices: 22.7 us -> 0.02 us  [body(): parts = lax.all_gather(d_branch, 'chan', axis=0, tiled=False)]
    convert_element_type x1, other arithmetic: 26.2 us -> 10.5 us  [body(): (cotangent.astype(jnp.float32) + depthwise(d_filtered, dw_kernel[::-1]))....]
    reduce_scatter x1, waiting for transfers between devices: 14.5 us -> 7.43 us  [body(): lax.psum_scatter(partial_normed.astype(jnp.bfloat16), 'chan', scatter_dim...]
    all_gather x1, waiting for transfers between devices: 22.3 us -> 18.3 us  [body(): gathered = lax.all_gather(normed, 'chan', axis=1, tiled=True)]
    all_gather x0 -> x1, local copies, waits for them, and re-layouts: none -> 4.01 us  [body(): parts = lax.all_gather(d_branch, 'chan', axis=0, tiled=False)]
    unnamed x29 -> x37, local copies, waits for them, and re-layouts: 12.1 us -> 10.2 us
  transfers between devices with their start and end apart: 5 -> 5, of which waited for: 4 -> 3; matrix products, arithmetic and copies ran while one was open for 18% -> 28% of each run, Pallas kernels for 0% -> 0%
where the time goes in v1:
time: 263 us; the launch traced here: 262 us
  blocking collectives  93.5 us (36%)
  waiting for transfers between devices  58.7 us (22%)
  other arithmetic  46.5 us (18%)
  matrix products  28.7 us (11%)
  local copies, waits for them, and re-layouts  20.2 us (8%)
  between operations  14.1 us (5%)
    psum x1, blocking collectives, body(): lax.psum((kernel_local, bias_local, scale_local), 'dp')  39.1 us
    unnamed x6, waiting for transfers between devices  33 us
    all_gather x1, blocking collectives, body(): per_device = lax.all_gather(moments[None], 'dp', axis=0, tiled=True)  27.9 us
    all_gather x1, blocking collectives, body(): grad_rows = lax.all_gather(grad_moments[None], 'dp', axis=0, tiled=True)  26.5 us
    all_gather x1, waiting for transfers between devices, body(): gathered = lax.all_gather(normed, 'chan', axis=1, tiled=True)  18.3 us
    convert_element_type x1, other arithmetic, body(): (cotangent.astype(jnp.float32) + depthwise(d_filtered, dw_kernel[::-1]))....  10.5 us
    unnamed x37, local copies, waits for them, and re-layouts  10.2 us
    reduce_sum x1, other arithmetic, body(): jnp.sum(filtered, axis=0)  9.63 us
  transfers between devices with their start and end apart: 5, of which 3 were waited for; matrix products, arithmetic and copies ran while one was open for 28% of the time, Pallas kernels for 0%

profile of v1, /device:TPU:0, one launch (start us, length us, event | category | flops | bytes accessed | tf_op | source)
XLA Modules:
  0.0 262.1 jit_solution(14346223415651264861)
XLA Ops:
  7.2 0.0 copy-start
  7.2 0.0 copy-start.7
  7.2 0.0 all-gather.9.cloned.1.call-start
  7.2 2.1 fusion.110
  9.3 0.0 all-gather.9.cloned.1.call-update
  9.4 0.0 copy-start.11
  9.4 0.0 copy-start.9
  9.4 0.0 copy-start.10
  9.4 0.0 all-gather.7.cloned.1.call-start
  9.5 1.0 fusion.122
  10.5 1.1 convert_element_type.94
  11.7 9.6 %fusion.118 = (f32[256]{0:T(256)S(1)}, f32[256]{0:T(256)S(1)}, f32[1,16,64,256]{3,2,1,0:T(8,128)}) fusion(f32[256]{0:T(256)S(1)} %bitcast.273, f32[256]{0:T(256)S(1)} %bitcast.275, f32[256]{0:T(256)S(1)} %bitcast.219, f32[256]{0:T(256)S(1)} %bitcast.221, f32[256]{0:T(256)S(1)} %bitcast.223, f32[256]{0:T(256)S(1)} %bitcast.225, f32[256]{0:T(256)S(1)} %bitcast.227, ...), kind=kLoop, calls=%fused_computation.304 | loop fusion | flops 26213888 | bytes 2149376 | tf_op jit(solution)/shard_map/reduce_sum | solution.py:66
  21.4 27.9 %all-gather.2 = f32[8,2,256]{2,1,0:T(2,128)S(1)} all-gather(f32[1,2,256]{2,1,0:T(2,128)S(1)} %maximum_bitcast_fusion), channel_id=2, replica_groups=mesh['dp'=8,'chan'=4] {'dp'}, dimensions={0}, use_global_device_ids=true | all-gather | bytes 18432 | tf_op jit(solution)/shard_map/all_gather | solution.py:67
  49.3 0.2 reduce-window.8
  49.5 0.6 fusion.117
  50.1 0.6 compare_convert_fusion.1
  50.8 0.1 convert_reduce_fusion.1
  50.8 0.1 multiply_reduce_fusion.51
  50.9 1.2 fusion.116
  52.2 0.1 multiply_reduce_fusion.57
  52.3 2.2 add_convert_fusion
  54.5 0.0 all-gather.7.cloned.1.call-update
  54.5 0.0 reduce-scatter.8.cloned.1.call-start
  54.6 0.0 all-gather.9.cloned.1.call-done
  54.6 4.0 %copy.28 = bf16[4,1024,256]{1,2,0:T(8,128)(2,1)} copy(bf16[4,1024,256]{2,1,0:T(8,128)(2,1)} %all-gather.9.cloned.1.call-done) | data formatting | bytes 4194304 | tf_op jit(solution)/shard_map/all_gather | solution.py:91
  58.6 18.3 %all-gather.7.cloned.1.call-done = bf16[1024,1024]{1,0:T(8,128)(2,1)} async-done(((bf16[1024,256]{1,0:T(8,128)(2,1)}), bf16[1024,1024]{1,0:T(8,128)(2,1)}) %all-gather.7.cloned.1.call-update) | async-done | bytes 2097168 | tf_op jit(solution)/shard_map/all_gather | solution.py:79
  76.9 4.7 %fusion.127 = f32[1024,1024]{1,0:T(8,128)S(1)} fusion(bf16[1024,1024]{1,0:T(8,128)(2,1)} %all-gather.7.cloned.1.call-done, bf16[1024,1024]{1,0:T(8,128)(2,1)} %param.15), kind=kOutput, calls=%fused_computation.311 | convolution fusion | flops 2147483648 | bytes 8388608 | tf_op jit(solution)/shard_map/dot_general | solution.py:80
  81.7 0.0 copy-start.12
  81.7 5.8 %fusion.119 = (f32[1024]{0:T(1024)}, bf16[1024,1024]{1,0:T(8,128)(2,1)S(1)}) fusion(f32[1024,1024]{1,0:T(8,128)S(1)} %fusion.127, f32[1024]{0:T(1024)S(1)} %copy-done.13, bf16[1024,1024]{0,1:T(8,128)(2,1)S(1)} %bitcast.214, bf16[1024,1024]{1,0:T(8,128)(2,1)S(1)} %copy-done), kind=kOutput, calls=%fused_computation.305 | convolution fusion | flops 2170551296 | bytes 10493952 | tf_op jit(solution)/shard_map/dot_general | solution.py:98
  87.4 1.4 copy-done.16
  88.8 3.7 %convolution_convert_fusion.2 = bf16[1024,1024]{1,0:T(8,128)(2,1)} fusion(bf16[1024,1024]{1,0:T(8,128)(2,1)S(1)} %copy-done.12, bf16[1024,1024]{1,0:T(8,128)(2,1)S(1)} %get-tuple-element.117), kind=kOutput, calls=%fused_computation.108 | convolution fusion | flops 2148532224 | bytes 6291456 | tf_op jit(solution)/shard_map/dot_general | solution.py:115
  92.5 0.0 reduce-scatter.8.cloned.1.call-update
  92.5 0.2 reduce-scatter.6.cloned.1.call-start
  92.7 6.4 %convolution_convert_fusion.3 = bf16[1024,1024]{1,0:T(8,128)(2,1)} fusion(bf16[1024,1024]{1,0:T(8,128)(2,1)S(1)} %copy-done, f32[1024,1024]{1,0:T(8,128)} %copy-done.14, f32[1024]{0:T(1024)S(1)} %copy-done.13), kind=kOutput, calls=%fused_computation.109 | convolution fusion | flops 2159017984 | bytes 8392704 | tf_op jit(solution)/shard_map/dot_general | solution.py:82
  99.1 0.0 reduce-scatter.6.cloned.1.call-update
  99.2 0.0 reduce-scatter.10.cloned.1.call-start
  99.2 5.2 %convolution_convert_fusion.1 = bf16[1024,1024]{0,1:T(8,128)(2,1)S(1)} fusion(bf16[1024,1024]{1,0:T(8,128)(2,1)} %all-gather.7.cloned.1.call-done, bf16[1024,1024]{1,0:T(8,128)(2,1)} %copy-done.16), kind=kOutput, calls=%fused_computation.107 | convolution fusion | flops 2148532224 | bytes 6291456 | tf_op jit(solution)/shard_map/dot_general | solution.py:105
  104.4 0.0 copy-done.6
  104.4 0.0 copy-done.15
  104.4 3.0 %convolution_convert_fusion = bf16[1024,1024]{0,1:T(8,128)(2,1)S(1)} fusion(bf16[1024,1024]{0,1:T(8,128)(2,1)S(1)} %bitcast.215, f32[1024,1024]{1,0:T(8,128)S(1)} %copy-done.15, f32[1024]{0:T(1024)S(1)} %copy-done.13), kind=kOutput, calls=%fused_computation.106 | convolution fusion | flops 2159017984 | bytes 8392704 | tf_op jit(solution)/shard_map/dot_general | solution.py:95
  107.4 2.4 pad_maximum_fusion
  109.9 6.5 %copy.33 = bf16[1024,2048]{1,0:T(8,128)(2,1)} copy(bf16[1024,2048]{0,1:T(8,128)(2,1)} %pad_maximum_fusion) | data formatting | bytes 8388608
  116.3 0.0 reduce-scatter.10.cloned.1.call-update
  116.4 7.4 %reduce-scatter.8.cloned.1.call-done = bf16[1024,256]{1,0:T(8,128)(2,1)} async-done(((bf16[1024,1024]{1,0:T(8,128)(2,1)}), bf16[1024,256]{1,0:T(8,128)(2,1)}) %reduce-scatter.8.cloned.1.call-update) | async-done | bytes 524304 | tf_op jit(solution)/shard_map/reduce_scatter | solution.py:118
  123.8 1.7 fusion.9
  125.5 0.0 copy-start.4
  125.6 26.5 %all-gather.3 = f32[8,2,256]{2,1,0:T(2,128)S(1)} all-gather(f32[1,2,256]{2,1,0:T(2,128)S(1)} %maximum_bitcast_fusion.1), channel_id=3, replica_groups=mesh['dp'=8,'chan'=4] {'dp'}, dimensions={0}, use_global_device_ids=true | all-gather | bytes 18432 | tf_op jit(solution)/shard_map/all_gather | solution.py:122
  152.1 0.1 multiply_reduce_fusion.50
  152.2 0.6 multiply_reduce_fusion.53
  152.8 0.6 broadcast_divide_fusion
  153.5 4.5 %multiply_reduce_fusion.1 = (f32[256]{0:T(256)S(1)}, f32[256]{0:T(256)S(1)}, f32[256]{0:T(256)S(1)}, f32[256]{0:T(256)S(1)}, f32[256]{0:T(256)S(1)}, /*index=5*/...) fusion(f32[1,16,64,256]{3,2,1,0:T(8,128)S(1)} %convert_element_, ...), kind=kLoop, calls=%fused_computation.224 | loop fusion | flops 11529728 | bytes 3693572 | tf_op jit(solution)/shard_map/reduce_sum | solution.py:30
  158.0 0.0 copy-start.8
  158.0 2.2 multiply_reduce_fusion.2
  160.2 2.3 multiply_reduce_fusion
  162.5 2.9 %stack.223 = f32[49,256]{1,0:T(8,128)S(1)} concatenate(f32[1,256]{1,0:T(1,128)} %bitcast.361, f32[1,256]{1,0:T(1,128)} %bitcast.360, f32[1,256]{1,0:T(1,128)} %bitcast.362, f32[1,256]{1,0:T(1,128)S(1)} %bitcast.316, f32[1,256]{1,0:T(1,128)S(1)} %bitcast.317, f32[1,256]{1,0:T(1,128)S(1)} %bitcast.318, f32[1,256]{1,0:T(1,128)S(1)} %bitcast.319, f32[1,256]{1,0:T(1,128)S(1)} %bitcast.320, ...), dimensions={0} | concatenate | bytes 100352 | tf_op jit(solution)/shard_map/stack | solution.py:31
  165.5 0.0 reduce-scatter.6.cloned.1.call-done
  165.5 2.4 fusion.8
  167.9 39.1 %all-reduce.2 = (f32[49,256]{1,0:T(8,128)}, f32[1024]{0:T(1024)}, f32[256]{0:T(256)}) all-reduce(f32[49,256]{1,0:T(8,128)S(1)} %stack.223, f32[1024]{0:T(1024)} %get-tuple-element.116, f32[256]{0:T(256)S(1)} %get-tuple-element.122), channel_id=1, replica_groups=mesh['dp'=8,'chan'=4] {'dp'}, use_global_device_ids=true, to_apply=%region_67.68 | all-reduce | flops 13824 | bytes 110592 | tf_op jit(solution)/shard_map/psum | solution.py:134
  207.0 10.5 %fusion.106 = bf16[1,16,64,256]{3,2,1,0:T(8,128)(2,1)} fusion(f32[1,16,64,256]{3,2,1,0:T(8,128)S(1)} %bitcast.213, f32[256]{0:T(256)S(1)} %bitcast.274, f32[256]{0:T(256)S(1)} %bitcast.276, f32[256]{0:T(256)S(1)} %bitcast.220, f32[256]{0:T(256)S(1)} %bitcast.222, f32[256]{0:T(256)S(1)} %bitcast.224, f32[256]{0:T(256)S(1)} %bitcast.226, ...), kind=kLoop, calls=%fused_computation.215 | loop fusion | flops 26214400 | bytes 2147328 | tf_op jit(solution)/shard_map/convert_element_type | solution.py:135
  217.4 32.9 %reduce-scatter.10.cloned.1.call-done = bf16[128,2048]{1,0:T(8,128)(2,1)} async-done(((bf16[1024,2048]{1,0:T(8,128)(2,1)}), bf16[128,2048]{1,0:T(8,128)(2,1)}) %reduce-scatter.10.cloned.1.call-update) | async-done | bytes 524304
  250.3 1.3 copy.34
  251.7 1.1 convert_element_type.113
  252.7 1.0 copy.32
  253.7 1.9 slice_bitcast_fusion
  (34 shorter events, 0.2 us)
Async XLA Ops:
  7.2 74.4 %copy-start = (bf16[1024,1024]{1,0:T(8,128)(2,1)S(1)}, bf16[1024,1024]{1,0:T(8,128)(2,1)}, u32[]{:S(2)}) copy-start(bf16[1024,1024]{1,0:T(8,128)(2,1)} %param.17) | copy-start | bytes 6291460
  7.2 4.5 %copy-start.7 = (f32[49,256]{1,0:T(8,128)S(1)}, f32[49,256]{1,0:T(8,128)}, u32[]{:S(2)}) copy-start(f32[49,256]{1,0:T(8,128)} %param.12) | copy-start | bytes 150532
  7.2 47.4 %all-gather.9.cloned.1.call-start = ((), (), s32[]{:S(2)}) async-start(), calls=%async_computation.5 | async-start | bytes 2621440 | tf_op jit(solution)/shard_map/all_gather | solution.py:91
  9.4 39.9 %copy-start.11 = (s32[4]{0:T(128)S(1)}, s32[4]{0:T(128)}, u32[]{:S(2)}) copy-start(s32[4]{0:T(128)} %param.19) | copy-start | bytes 52
  9.4 42.8 %copy-start.9 = (f32[4,256]{1,0:T(4,128)S(1)}, f32[4,256]{1,0:T(4,128)}, u32[]{:S(2)}) copy-start(f32[4,256]{1,0:T(4,128)} %param.13) | copy-start | bytes 12292
  9.4 42.8 %copy-start.10 = (f32[4,256]{1,0:T(4,128)S(1)}, f32[4,256]{1,0:T(4,128)}, u32[]{:S(2)}) copy-start(f32[4,256]{1,0:T(4,128)} %param.14) | copy-start | bytes 12292
  9.4 67.5 %all-gather.7.cloned.1.call-start = ((), (), s32[]{:S(2)}) async-start(), calls=%async_computation.3 | async-start | bytes 2621440 | tf_op jit(solution)/shard_map/all_gather | solution.py:79
  54.5 69.3 %reduce-scatter.8.cloned.1.call-start = ((), (), s32[]{:S(2)}) async-start(), calls=%async_computation.6 | async-start | bytes 2621440 | tf_op jit(solution)/shard_map/reduce_scatter | solution.py:118
  58.6 23.0 %copy-start.13 = (f32[1024]{0:T(1024)S(1)}, f32[1024]{0:T(1024)}, u32[]{:S(2)}) copy-start(f32[1024]{0:T(1024)} %param.16) | copy-start | bytes 12292
  76.9 4.7 %copy-start.5 = (bf16[4,1024,256]{1,2,0:T(8,128)(2,1)S(1)}, bf16[4,1024,256]{1,2,0:T(8,128)(2,1)}, u32[]{:S(2)}) copy-start(bf16[4,1024,256]{1,2,0:T(8,128)(2,1)} %copy.28) | copy-start | bytes 6291460
  81.6 5.8 %copy-start.14 = (f32[1024,1024]{1,0:T(8,128)}, f32[1024,1024]{1,0:T(8,128)S(1)}, u32[]{:S(2)}) copy-start(f32[1024,1024]{1,0:T(8,128)S(1)} %fusion.127) | copy-start | bytes 12582916
  81.7 7.1 %copy-start.12 = (bf16[1024,1024]{1,0:T(8,128)(2,1)S(1)}, bf16[1024,1024]{1,0:T(8,128)(2,1)}, u32[]{:S(2)}) copy-start(bf16[1024,1024]{1,0:T(8,128)(2,1)} %param.15) | copy-start | bytes 6291460
  87.4 1.4 copy-start.16
  92.5 73.0 %reduce-scatter.6.cloned.1.call-start = ((), (), s32[]{:S(2)}) async-start(), calls=%async_computation.4 | async-start | bytes 2621440 | tf_op jit(solution)/shard_map/reduce_scatter | solution.py:83
  99.2 151.2 %reduce-scatter.10.cloned.1.call-start = ((), (), s32[]{:S(2)}) async-start(), calls=%async_computation.7 | async-start | bytes 4718592
  99.2 5.2 %copy-start.6 = (bf16[4,1024,256]{1,2,0:T(8,128)(2,1)S(1)}, bf16[4,1024,256]{1,2,0:T(8,128)(2,1)}, u32[]{:S(2)}) copy-start(bf16[4,1024,256]{1,2,0:T(8,128)(2,1)} %copy.28) | copy-start | bytes 6291460
  99.2 5.2 %copy-start.15 = (f32[1024,1024]{1,0:T(8,128)S(1)}, f32[1024,1024]{1,0:T(8,128)}, u32[]{:S(2)}) copy-start(f32[1024,1024]{1,0:T(8,128)} %copy-done.14) | copy-start | bytes 12582916
  123.8 29.7 %copy-start.1 = (f32[1,16,64,256]{3,2,1,0:T(8,128)S(1)}, f32[1,16,64,256]{3,2,1,0:T(8,128)}, u32[]{:S(2)}) copy-start(f32[1,16,64,256]{3,2,1,0:T(8,128)} %get-tuple-element.121) | copy-start | bytes 3145732
  125.5 32.4 %copy-start.4 = (bf16[1,16,64,256]{3,2,1,0:T(8,128)(2,1)S(1)}, bf16[1,16,64,256]{3,2,1,0:T(8,128)(2,1)}, u32[]{:S(2)}) copy-start(bf16[1,16,64,256]{3,2,1,0:T(8,128)(2,1)} %param.10) | copy-start | bytes 1572868
  158.0 4.5 %copy-start.2 = (f32[1024,256]{1,0:T(8,128)}, f32[1024,256]{1,0:T(8,128)S(1)}, u32[]{:S(2)}) copy-start(f32[1024,256]{1,0:T(8,128)S(1)} %get-tuple-element.118) | copy-start | bytes 3145732
  158.0 7.5 %copy-start.8 = (f32[256]{0:T(256)S(1)}, f32[256]{0:T(256)}, u32[]{:S(2)}) copy-start(f32[256]{0:T(256)} %param.18) | copy-start | bytes 3076
  162.5 44.5 %copy-start.3 = (f32[1024,256]{1,0:T(8,128)S(1)}, f32[1024,256]{1,0:T(8,128)}, u32[]{:S(2)}) copy-start(f32[1024,256]{1,0:T(8,128)} %copy-done.2) | copy-start | bytes 3145732
Sparse Core Ops, SparseCore 0:
  10.1 25.2 all-gather.8
  54.7 22.2 all-gather.6
  92.6 31.1 reduce-scatter.7
  126.2 31.1 reduce-scatter.5
  160.9 89.4 reduce-scatter.9
